TPU v7x, 32 devices: a whole 2x2x4 slice. The times are simulated.
32 devices in a mesh: expert: 8 (over z, y), dp: 4 (over x, core).
Axes of the slice: x: 2, y: 2, z: 4, core: 2. Of those that a mesh axis runs over, the one named last changes fastest.
Arguments:
- grad_parts: bfloat16 [4, 8, 3584, 1024], P('dp', 'expert'), may hold values from -6 to 6
- owner_slot: int32 [8], replicated, may hold values from 0 to 7, each once
- slot_expert: int32 [8, 2], replicated, may hold values from 0 to 7, all different within a row
- master: float32 [8, 3584, 1024], P(None, 'expert', 'dp'), may hold values from -1.5 to 1.5
- moment_one: float32 [8, 3584, 1024], P(None, 'expert', 'dp'), may hold values from -2 to 2
- moment_two: float32 [8, 3584, 1024], P(None, 'expert', 'dp'), may hold values from 0.01 to 1
- ema_weights: float32 [8, 3584, 1024], P(None, 'expert', 'dp'), may hold values from -1.5 to 1.5
Outputs:
- master_out: float32 [8, 3584, 1024], P(None, 'expert', 'dp')
- moment_one_out: float32 [8, 3584, 1024], P(None, 'expert', 'dp')
- moment_two_out: float32 [8, 3584, 1024], P(None, 'expert', 'dp')
- ema_out: float32 [8, 3584, 1024], P(None, 'expert', 'dp')
- replicas: bfloat16 [16, 3584, 1024], P('expert', None, 'dp')
Inputs may be any that keep to these rules, and one draw needn't show every extreme that they name: `owner_slot`: a permutation of the 8 experts; position k belongs to expert-axis index k. `slot_expert`: each row names 2 different experts, and every expert is named by some row.
All inputs are finite; a program needn't handle non-finite values.
Results may differ from a plain program's by a relative error of at most 0.009.
Values may be sent and summed in bfloat16 or wider, within the bound.
A program may use at most 128 MiB of HBM per device.

v0:
```python
import jax
import jax.numpy as jnp
from jax import lax
from jax.sharding import PartitionSpec as P

STEP = 10
beta_one = 0.9
beta_two = 0.999
adam_eps = 1e-08
learn_rate = 0.05
decay_rate = 0.1
ema_decay = 0.99


def per_device(grad_parts, owner_slot, slot_expert, master, moment_one, moment_two, ema_weights):
    summed = lax.psum_scatter(
        grad_parts[0].astype(jnp.float32).astype(jnp.bfloat16),
        "dp",
        scatter_dimension=2,
        tiled=True,
    ).astype(jnp.float32)
    owner_rows = lax.all_to_all(
        summed.astype(jnp.bfloat16), "expert", split_axis=1, concat_axis=0, tiled=True
    ).astype(summed.dtype)
    gradient = jnp.take(owner_rows, owner_slot, axis=0)
    correct_one = 1.0 - beta_one**STEP
    correct_two = 1.0 - beta_two**STEP
    moment_one_out = beta_one * moment_one + (1.0 - beta_one) * gradient
    moment_two_out = beta_two * moment_two + (1.0 - beta_two) * gradient * gradient
    update = moment_one_out / correct_one / (jnp.sqrt(moment_two_out / correct_two) + adam_eps)
    master_out = master - learn_rate * (update + decay_rate * master)
    ema_out = ema_decay * ema_weights + (1.0 - ema_decay) * master_out
    updated_bf16 = master_out.astype(jnp.bfloat16)
    outgoing = jnp.take(updated_bf16, slot_expert.reshape(-1), axis=0)
    replicas = lax.all_to_all(outgoing, "expert", split_axis=0, concat_axis=1, tiled=True)
    return (master_out, moment_one_out, moment_two_out, ema_out, replicas)


def solution(mesh):
    placed = (
        P("dp", "expert", None, None),
        P(),
        P(),
        P(None, "expert", "dp"),
        P(None, "expert", "dp"),
        P(None, "expert", "dp"),
        P(None, "expert", "dp"),
    )
    return jax.shard_map(
        per_device,
        mesh=mesh,
        in_specs=placed,
        out_specs=(
            P(None, "expert", "dp"),
            P(None, "expert", "dp"),
            P(None, "expert", "dp"),
            P(None, "expert", "dp"),
            P("expert", None, "dp"),
        ),
        check_vma=False,
    )
```

profile of v0, /device:TPU:0, one launch (start us, length us, event | category | flops | bytes accessed | tf_op | source)
XLA Modules:
  0.0 281.6 jit_solution(11911839623130922514)
XLA Ops:
  7.2 0.0 reduce-scatter.2.cloned.1.call-start
  7.2 0.7 reduce-scatter.2.cloned.1.call-update
  7.9 69.9 %reduce-scatter.2.cloned.1.call-done = bf16[1,3584,256]{2,1,0:T(8,128)(2,1)} async-done(((bf16[1,3584,1024]{2,1,0:T(8,128)(2,1)}), bf16[1,3584,256]{2,1,0:T(8,128)(2,1)}) %reduce-scatter.2.cloned.1.call-update) | async-done | bytes 1835024 | tf_op jit(solution)/shard_map/reduce_scatter | solution.py:16
  77.8 6.8 %copy.27 = bf16[1,3584,256]{2,0,1:T(2,128)(2,1)} copy(bf16[1,3584,256]{2,1,0:T(8,128)(2,1)} %reduce-scatter.2.cloned.1.call-done) | data formatting | bytes 3670016 | tf_op jit(solution)/shard_map/reduce_scatter | solution.py:16
  84.6 0.5 broadcast.61
  85.1 19.1 %reduce = bf16[3584,256]{1,0:T(8,128)(2,1)S(1)} reduce(bf16[3584,1,256]{2,1,0:T(2,128)(2,1)} %bitcast.14, bf16[]{:T(256)} %broadcast.61), dimensions={1}, to_apply=%bitcast.11.reduce_sub_computation | reduce | bytes 3670018
  104.2 0.0 copy-start
  104.2 0.0 copy-start.1
  104.2 3.1 %reshape.79 = bf16[8,2,57344]{2,1,0:T(2,128)(2,1)} reshape(bf16[3584,256]{1,0:T(8,128)(2,1)S(1)} %reduce) | data formatting | bytes 3670016
  107.3 5.5 %all-to-all-start = ((bf16[8,2,57344]{2,1,0:T(2,128)(2,1)}), bf16[8,2,57344]{2,1,0:T(2,128)(2,1)S(1)}, u32[]{:S(2)}, u32[]{:S(2)}) async-start(bf16[8,2,57344]{2,1,0:T(2,128)(2,1)} %reshape.79), calls=%async_computation.1 | async-start | bytes 3670016 | tf_op jit(solution)/shard_map/all_to_all | solution.py:22
  112.8 0.0 copy-done
  112.9 0.1 copy.22
  112.9 0.1 reshape.60
  113.0 0.1 reshape.59
  113.1 0.0 copy-done.1
  113.2 42.2 %all-to-all-done = bf16[8,2,57344]{2,1,0:T(2,128)(2,1)S(1)} async-done(((bf16[8,2,57344]{2,1,0:T(2,128)(2,1)}), bf16[8,2,57344]{2,1,0:T(2,128)(2,1)S(1)}, u32[]{:S(2)}, u32[]{:S(2)}) %all-to-all-start) | async-done | bytes 1835040 | tf_op jit(solution)/shard_map/all_to_all | solution.py:22
  155.3 4.1 %reshape.80 = bf16[3584,1,256]{2,1,0:T(2,128)(2,1)} reshape(bf16[8,2,57344]{2,1,0:T(2,128)(2,1)S(1)} %all-to-all-done) | data formatting | bytes 3670016
  159.4 4.1 %copy.25 = f32[1,3584,256]{2,1,0:T(8,128)} copy(bf16[1,3584,256]{2,0,1:T(2,128)(2,1)} %bitcast.13) | data formatting | bytes 5505024
  163.5 4.7 %gather_fusion = f32[8,448,256]{2,1,0:T(8,128)} fusion(f32[8,448,256]{2,1,0:T(8,128)} %bitcast.12, s32[1024]{0:T(1024)S(1)} %pad_clamp_fusion.1), kind=kCustom, calls=%fused_computation | custom fusion | bytes 7340064 | tf_op jit(solution)/shard_map/jit(_take)/gather | solution.py:25
  168.2 9.6 %fusion.2 = (bf16[8,448,256]{2,1,0:T(8,128)(2,1)S(1)}, f32[8,448,256]{2,1,0:T(8,128)}, f32[8,448,256]{2,1,0:T(8,128)}, f32[8,448,256]{2,1,0:T(8,128)}) fusion(f32[8,448,256]{2,1,0:T(8,128)} %param.10, f32[8,448,256]{2,1,0:T(8,128)} %gather_fusion, pred[8]{0:T(512)(128)(4,1)S(1)} %compare_and_fusion.1, f32[8,448,256]{2,1,0:T(8,128)} %param.11, ...), kind=kLoop, calls=%fused_computation.16 | loop fusion | flops 15597568 | bytes 27525128 | tf_op jit(solution)/shard_map/convert_element_type | solution.py:33
  177.7 2.6 gather_fusion.1
  180.4 4.3 %broadcast_select_fusion = bf16[16,448,256]{2,1,0:T(8,128)(2,1)} fusion(bf16[16,448,256]{2,1,0:T(8,128)(2,1)} %gather_fusion.1, pred[16]{0:T(512)(128)(4,1)S(1)} %compare_and_fusion), kind=kLoop, calls=%fused_computation.7 | loop fusion | flops 1835008 | bytes 7340048 | tf_op jit(solution)/shard_map/jit(_take)/select_n | solution.py:34
  184.6 4.5 %all-to-all-start.1 = ((bf16[16,448,256]{2,1,0:T(8,128)(2,1)}), bf16[16,448,256]{2,1,0:T(8,128)(2,1)}, u32[]{:S(2)}, u32[]{:S(2)}) async-start(bf16[16,448,256]{2,1,0:T(8,128)(2,1)} %broadcast_select_fusion), calls=%async_computation.2 | async-start | bytes 7340032 | tf_op jit(solution)/shard_map/all_to_all | solution.py:35
  189.1 5.6 %multiply_add_fusion = f32[8,448,256]{2,1,0:T(8,128)} fusion(f32[8,448,256]{2,1,0:T(8,128)} %get-tuple-element.6, f32[8,448,256]{2,1,0:T(8,128)} %param.13), kind=kLoop, calls=%fused_computation.4 | loop fusion | flops 2752512 | bytes 11010048 | tf_op jit(solution)/shard_map/add | solution.py:32
  194.7 75.8 %all-to-all-done.1 = bf16[16,448,256]{2,1,0:T(8,128)(2,1)} async-done(((bf16[16,448,256]{2,1,0:T(8,128)(2,1)}), bf16[16,448,256]{2,1,0:T(8,128)(2,1)}, u32[]{:S(2)}, u32[]{:S(2)}) %all-to-all-start.1) | async-done | bytes 3670048 | tf_op jit(solution)/shard_map/all_to_all | solution.py:35
  270.5 4.2 %copy.24 = bf16[2,8,448,256]{3,2,1,0:T(8,128)(2,1)} copy(bf16[2,8,448,256]{3,2,0,1:T(8,128)(2,1)} %bitcast.3) | data formatting | bytes 7340032 | tf_op jit(solution)/shard_map/all_to_all | solution.py:35
  (6 shorter events, 0.0 us)
Async XLA Ops:
  7.2 70.7 %reduce-scatter.2.cloned.1.call-start = ((), (), s32[]{:S(2)}) async-start(), calls=%async_computation.3 | async-start | bytes 9175040 | tf_op jit(solution)/shard_map/reduce_scatter | solution.py:16
  104.2 8.6 %copy-start = (s32[8,2]{0,1:T(2,128)S(1)}, s32[8,2]{0,1:T(2,128)}, u32[]{:S(2)}) copy-start(s32[8,2]{0,1:T(2,128)} %param.9) | copy-start | bytes 196
  104.2 8.9 %copy-start.1 = (s32[8]{0:T(128)S(1)}, s32[8]{0:T(128)}, u32[]{:S(2)}) copy-start(s32[8]{0:T(128)} %param.8) | copy-start | bytes 100
  107.3 48.0 %all-to-all-start = ((bf16[8,2,57344]{2,1,0:T(2,128)(2,1)}), bf16[8,2,57344]{2,1,0:T(2,128)(2,1)S(1)}, u32[]{:S(2)}, u32[]{:S(2)}) async-start(bf16[8,2,57344]{2,1,0:T(2,128)(2,1)} %reshape.79), calls=%async_computation.1 | async-start | bytes 3670016 | tf_op jit(solution)/shard_map/all_to_all | solution.py:22
  184.6 85.9 %all-to-all-start.1 = ((bf16[16,448,256]{2,1,0:T(8,128)(2,1)}), bf16[16,448,256]{2,1,0:T(8,128)(2,1)}, u32[]{:S(2)}, u32[]{:S(2)}) async-start(bf16[16,448,256]{2,1,0:T(8,128)(2,1)} %broadcast_select_fusion), calls=%async_computation.2 | async-start | bytes 7340032 | tf_op jit(solution)/shard_map/all_to_all | solution.py:35
Sparse Core Ops, SparseCore 0:
  10.5 67.2 reduce-scatter.1
where the time goes:
time: 282 us
  waiting for transfers between devices  189 us (67%)
  other arithmetic  38.6 us (14%)
  local copies, waits for them, and re-layouts  30.3 us (11%)
  between operations  14.1 us (5%)
  starting transfers between devices  10 us (4%)
    all_to_all x1, waiting for transfers between devices, per_device(): lax.all_to_all(outgoing, 'expert', split_axis=0, concat_axis=1, tiled=True)  75.8 us
    reduce_scatter x1, waiting for transfers between devices, per_device(): lax.psum_scatter(grad_parts[0].astype(jnp.float32).astype(jnp.bfloat16),...  69.9 us
    all_to_all x1, waiting for transfers between devices, per_device(): lax.all_to_all(summed.astype(jnp.bfloat16), 'expert', split_axis=1, conca...  42.2 us
    unnamed x1, other arithmetic  19.1 us
    unnamed x9, local copies, waits for them, and re-layouts  11.9 us
    convert_element_type x1, other arithmetic, per_device(): updated_bf16 = master_out.astype(jnp.bfloat16)  9.56 us
    reduce_scatter x1, local copies, waits for them, and re-layouts, per_device(): lax.psum_scatter(grad_parts[0].astype(jnp.float32).astype(jnp.bfloat16),...  6.77 us
  transfers between devices with their start and end apart: 3, of which 3 were waited for; matrix products, arithmetic and copies ran while one was open for 2% of the time, Pallas kernels for 0%

commit v1 on v0

--- a/solution.py
+++ b/solution.py
@@ -12,6 +12,18 @@
 ema_decay = 0.99
 
 
+def exchange_directly(x, axis, split, join):
+    ways, here = (lax.axis_size(axis), lax.axis_index(axis))
+    width = x.shape[split] // ways
+    turned = jnp.roll(x, -here * width, axis=split)
+    got = [lax.slice_in_dim(turned, 0, width, axis=split)]
+    for far in range(1, ways):
+        sent = lax.slice_in_dim(turned, far * width, (far + 1) * width, axis=split)
+        got.append(lax.ppermute(sent, axis, [(d, (d + far) % ways) for d in range(ways)]))
+    line = jnp.concatenate(got[::-1], axis=join)
+    return jnp.roll(line, (here + 1) * got[0].shape[join], axis=join)
+
+
 def per_device(grad_parts, owner_slot, slot_expert, master, moment_one, moment_two, ema_weights):
     summed = lax.psum_scatter(
         grad_parts[0].astype(jnp.float32).astype(jnp.bfloat16),
@@ -19,9 +31,7 @@
         scatter_dimension=2,
         tiled=True,
     ).astype(jnp.float32)
-    owner_rows = lax.all_to_all(
-        summed.astype(jnp.bfloat16), "expert", split_axis=1, concat_axis=0, tiled=True
-    ).astype(summed.dtype)
+    owner_rows = exchange_directly(summed.astype(jnp.bfloat16), "expert", 1, 0).astype(summed.dtype)
     gradient = jnp.take(owner_rows, owner_slot, axis=0)
     correct_one = 1.0 - beta_one**STEP
     correct_two = 1.0 - beta_two**STEP

time: 282 us -> 247 us (0.88)
  local copies, waits for them, and re-layouts: 30.3 us -> 12.1 us
  other arithmetic: 38.6 us -> 24.7 us
  waiting for transfers between devices: 189 us -> 179 us
  starting transfers between devices: 10 us -> 16.8 us
    all_to_all x1 -> x0, waiting for transfers between devices: 42.2 us -> none  [per_device(): lax.all_to_all(summed.astype(jnp.bfloat16), 'expert', split_axis=1, conca...]
    ppermute x0 -> x7, waiting for transfers between devices: none -> 32.2 us  [exchange_directly(): lax.ppermute(sent, axis, [(d, (d + far) % ways) for d in range(ways)])]
    unnamed x1 -> x0, other arithmetic: 19.1 us -> none
    unnamed x9 -> x20, local copies, waits for them, and re-layouts: 11.9 us -> 0.34 us
    ppermute x0 -> x7, starting transfers between devices: none -> 11.2 us  [exchange_directly(): lax.ppermute(sent, axis, [(d, (d + far) % ways) for d in range(ways)])]
    reduce_scatter x1 -> x0, local copies, waits for them, and re-layouts: 6.77 us -> none  [per_device(): lax.psum_scatter(grad_parts[0].astype(jnp.float32).astype(jnp.bfloat16),...]
    all_to_all x1 -> x0, starting transfers between devices: 5.52 us -> none  [per_device(): lax.all_to_all(summed.astype(jnp.bfloat16), 'expert', split_axis=1, conca...]
    concatenate x0 -> x1, other arithmetic: none -> 3.09 us  [exchange_directly(): turned = jnp.roll(x, -here * width, axis=split)]
  transfers between devices with their start and end apart: 3 -> 9, of which waited for: 3 -> 6; matrix products, arithmetic and copies ran while one was open for 2% -> 2% of each run, Pallas kernels for 0% -> 0%
where the time goes in v1:
time: 247 us
  waiting for transfers between devices  179 us (72%)
  other arithmetic  24.7 us (10%)
  starting transfers between devices  16.8 us (7%)
  between operations  14.3 us (6%)
  local copies, waits for them, and re-layouts  12.1 us (5%)
    all_to_all x1, waiting for transfers between devices, per_device(): lax.all_to_all(outgoing, 'expert', split_axis=0, concat_axis=1, tiled=True)  76.7 us
    reduce_scatter x1, waiting for transfers between devices, per_device(): lax.psum_scatter(grad_parts[0].astype(jnp.float32).astype(jnp.bfloat16),...  69.6 us
    ppermute x7, waiting for transfers between devices, exchange_directly(): lax.ppermute(sent, axis, [(d, (d + far) % ways) for d in range(ways)])  32.2 us
    ppermute x7, starting transfers between devices, exchange_directly(): lax.ppermute(sent, axis, [(d, (d + far) % ways) for d in range(ways)])  11.2 us
    convert_element_type x1, other arithmetic, per_device(): updated_bf16 = master_out.astype(jnp.bfloat16)  9.56 us
    all_to_all x1, starting transfers between devices, per_device(): lax.all_to_all(outgoing, 'expert', split_axis=0, concat_axis=1, tiled=True)  5.61 us
    add x1, other arithmetic, per_device(): ema_out = ema_decay * ema_weights + (1.0 - ema_decay) * master_out  5.58 us
  transfers between devices with their start and end apart: 9, of which 6 were waited for; matrix products, arithmetic and copies ran while one was open for 2% of the time, Pallas kernels for 0%

profile of v1, /device:TPU:0, one launch (start us, length us, event | category | flops | bytes accessed | tf_op | source)
XLA Modules:
  0.0 247.0 jit_solution(2521211663224226463)
XLA Ops:
  7.2 0.0 reduce-scatter.2.cloned.1.call-start
  7.2 0.7 reduce-scatter.2.cloned.1.call-update
  7.9 0.0 copy-done
  7.9 0.1 copy.15
  8.0 0.1 reshape.55
  8.1 0.1 reshape.54
  8.2 69.6 %reduce-scatter.2.cloned.1.call-done = bf16[1,3584,256]{2,1,0:T(8,128)(2,1)} async-done(((bf16[1,3584,1024]{2,1,0:T(8,128)(2,1)}), bf16[1,3584,256]{2,1,0:T(8,128)(2,1)}) %reduce-scatter.2.cloned.1.call-update) | async-done | bytes 1835024 | tf_op jit(solution)/shard_map/reduce_scatter | solution.py:28
  77.8 3.1 %fusion.1 = bf16[1,3584,256]{2,1,0:T(8,128)(2,1)S(1)} fusion(s32[]{:T(128)S(6)} %select_n.54, bf16[1,3584,256]{2,1,0:T(8,128)(2,1)} %reduce-scatter.2.cloned.1.call-done), kind=kLoop, calls=%fused_computation.10 | loop fusion | flops 3670016 | bytes 3670020 | tf_op jit(solution)/shard_map/jit(_roll_dynamic)/concatenate | solution.py:18
  80.9 0.1 fusion.5
  81.1 4.4 %collective-permute-start = (bf16[1,448,256]{2,1,0:T(8,128)(2,1)S(1)}, bf16[1,448,256]{2,1,0:T(8,128)(2,1)S(1)}, u32[]{:S(2)}, u32[]{:S(2)}) collective-permute-start(bf16[1,448,256]{2,1,0:T(8,128)(2,1)S(1)} %get-tuple-element.15), channel_id=1, source_target_pairs={{0,28},{4,0},{8,4},{12,8},{16,12},{20,16},{24,20},{28,24},{1,29},{... | collective-permute-start | bytes 688136 | tf_op jit(solution)/shard_map/ppermute | solution.py:22
  85.4 0.5 collective-permute-start.1
  85.9 0.6 collective-permute-start.6
  86.5 1.0 collective-permute-start.5
  87.5 0.9 collective-permute-start.4
  88.4 3.0 %collective-permute-done = bf16[1,448,256]{2,1,0:T(8,128)(2,1)S(1)} collective-permute-done((bf16[1,448,256]{2,1,0:T(8,128)(2,1)S(1)}, bf16[1,448,256]{2,1,0:T(8,128)(2,1)S(1)}, u32[]{:S(2)}, u32[]{:S(2)}) %collective-permute-start) | collective-permute-done | bytes 229408 | tf_op jit(solution)/shard_map/ppermute | solution.py:22
  91.4 2.4 collective-permute-start.2
  93.8 2.5 %collective-permute-done.1 = bf16[1,448,256]{2,1,0:T(8,128)(2,1)S(1)} collective-permute-done((bf16[1,448,256]{2,1,0:T(8,128)(2,1)S(1)}, bf16[1,448,256]{2,1,0:T(8,128)(2,1)S(1)}, u32[]{:S(2)}, u32[]{:S(2)}) %collective-permute-start.1) | collective-permute-done | bytes 229408 | tf_op jit(solution)/shard_map/ppermute | solution.py:22
  96.4 1.5 collective-permute-start.3
  97.8 13.3 %collective-permute-done.2 = bf16[1,448,256]{2,1,0:T(8,128)(2,1)S(1)} collective-permute-done((bf16[1,448,256]{2,1,0:T(8,128)(2,1)S(1)}, bf16[1,448,256]{2,1,0:T(8,128)(2,1)S(1)}, u32[]{:S(2)}, u32[]{:S(2)}) %collective-permute-start.2) | collective-permute-done | bytes 229408 | tf_op jit(solution)/shard_map/ppermute | solution.py:22
  111.2 13.3 %collective-permute-done.3 = bf16[1,448,256]{2,1,0:T(8,128)(2,1)S(1)} collective-permute-done((bf16[1,448,256]{2,1,0:T(8,128)(2,1)S(1)}, bf16[1,448,256]{2,1,0:T(8,128)(2,1)S(1)}, u32[]{:S(2)}, u32[]{:S(2)}) %collective-permute-start.3) | collective-permute-done | bytes 229408 | tf_op jit(solution)/shard_map/ppermute | solution.py:22
  124.5 0.0 collective-permute-done.4
  124.5 0.0 collective-permute-done.5
  124.6 0.0 collective-permute-done.6
  124.8 2.2 dynamic-slice_convert_fusion
  127.0 4.7 %gather_fusion = f32[8,448,256]{2,1,0:T(8,128)} fusion(f32[8,448,256]{2,1,0:T(8,128)} %dynamic-slice_convert_fusion, s32[1024]{0:T(1024)S(1)} %get-tuple-element.17), kind=kCustom, calls=%fused_computation | custom fusion | bytes 7340064 | tf_op jit(solution)/shard_map/jit(_take)/gather | solution.py:35
  131.7 9.6 %fusion.3 = (bf16[8,448,256]{2,1,0:T(8,128)(2,1)S(1)}, f32[8,448,256]{2,1,0:T(8,128)}, f32[8,448,256]{2,1,0:T(8,128)}, f32[8,448,256]{2,1,0:T(8,128)}) fusion(f32[8,448,256]{2,1,0:T(8,128)} %param.10, f32[8,448,256]{2,1,0:T(8,128)} %gather_fusion, pred[8]{0:T(512)(128)(4,1)S(1)} %compare_and_fusion.1, f32[8,448,256]{2,1,0:T(8,128)} %param.11, ...), kind=kLoop, calls=%fused_computation.36 | loop fusion | flops 15597568 | bytes 27525128 | tf_op jit(solution)/shard_map/convert_element_type | solution.py:43
  141.2 2.6 %gather_fusion.1 = bf16[16,448,256]{2,1,0:T(8,128)(2,1)} fusion(bf16[8,448,256]{2,1,0:T(8,128)(2,1)S(1)} %get-tuple-element.5, s32[1024]{0:T(1024)S(1)} %get-tuple-element.16), kind=kCustom, calls=%fused_computation.1 | custom fusion | bytes 7340096 | tf_op jit(solution)/shard_map/jit(_take)/gather | solution.py:44
  143.8 4.3 %broadcast_select_fusion = bf16[16,448,256]{2,1,0:T(8,128)(2,1)} fusion(bf16[16,448,256]{2,1,0:T(8,128)(2,1)} %gather_fusion.1, pred[16]{0:T(512)(128)(4,1)S(1)} %compare_and_fusion), kind=kLoop, calls=%fused_computation.9 | loop fusion | flops 1835008 | bytes 7340048 | tf_op jit(solution)/shard_map/jit(_take)/select_n | solution.py:44
  148.1 5.6 %all-to-all-start = ((bf16[16,448,256]{2,1,0:T(8,128)(2,1)}), bf16[16,448,256]{2,1,0:T(8,128)(2,1)}, u32[]{:S(2)}, u32[]{:S(2)}) async-start(bf16[16,448,256]{2,1,0:T(8,128)(2,1)} %broadcast_select_fusion), calls=%async_computation.1 | async-start | bytes 7340032 | tf_op jit(solution)/shard_map/all_to_all | solution.py:45
  153.7 5.6 %multiply_add_fusion = f32[8,448,256]{2,1,0:T(8,128)} fusion(f32[8,448,256]{2,1,0:T(8,128)} %get-tuple-element.6, f32[8,448,256]{2,1,0:T(8,128)} %param.13), kind=kLoop, calls=%fused_computation.6 | loop fusion | flops 2752512 | bytes 11010048 | tf_op jit(solution)/shard_map/add | solution.py:42
  159.3 76.7 %all-to-all-done = bf16[16,448,256]{2,1,0:T(8,128)(2,1)} async-done(((bf16[16,448,256]{2,1,0:T(8,128)(2,1)}), bf16[16,448,256]{2,1,0:T(8,128)(2,1)}, u32[]{:S(2)}, u32[]{:S(2)}) %all-to-all-start) | async-done | bytes 3670048 | tf_op jit(solution)/shard_map/all_to_all | solution.py:45
  236.0 4.2 %copy.17 = bf16[2,8,448,256]{3,2,1,0:T(8,128)(2,1)} copy(bf16[2,8,448,256]{3,2,0,1:T(8,128)(2,1)} %bitcast.3) | data formatting | bytes 7340032 | tf_op jit(solution)/shard_map/all_to_all | solution.py:45
  (24 shorter events, 0.3 us)
Async XLA Ops:
  7.2 70.7 %reduce-scatter.2.cloned.1.call-start = ((), (), s32[]{:S(2)}) async-start(), calls=%async_computation.2 | async-start | bytes 9175040 | tf_op jit(solution)/shard_map/reduce_scatter | solution.py:28
  7.2 0.7 copy-start
  7.2 1.0 copy-start.1
  81.1 10.4 %collective-permute-start = (bf16[1,448,256]{2,1,0:T(8,128)(2,1)S(1)}, bf16[1,448,256]{2,1,0:T(8,128)(2,1)S(1)}, u32[]{:S(2)}, u32[]{:S(2)}) collective-permute-start(bf16[1,448,256]{2,1,0:T(8,128)(2,1)S(1)} %get-tuple-element.15), channel_id=1, source_target_pairs={{0,28},{4,0},{8,4},{12,8},{16,12},{20,16},{24,20},{28,24},{1,29},{... | collective-permute-start | bytes 688136 | tf_op jit(solution)/shard_map/ppermute | solution.py:22
  85.4 10.9 %collective-permute-start.1 = (bf16[1,448,256]{2,1,0:T(8,128)(2,1)S(1)}, bf16[1,448,256]{2,1,0:T(8,128)(2,1)S(1)}, u32[]{:S(2)}, u32[]{:S(2)}) collective-permute-start(bf16[1,448,256]{2,1,0:T(8,128)(2,1)S(1)} %get-tuple-element.14), channel_id=1, source_target_pairs={{0,24},{4,28},{8,0},{12,4},{16,8},{20,12},{24,16},{28,20},{1,25},{... | collective-permute-start | bytes 688136 | tf_op jit(solution)/shard_map/ppermute | solution.py:22
  85.9 38.7 %collective-permute-start.6 = (bf16[1,448,256]{2,1,0:T(8,128)(2,1)S(1)}, bf16[1,448,256]{2,1,0:T(8,128)(2,1)S(1)}, u32[]{:S(2)}, u32[]{:S(2)}) collective-permute-start(bf16[1,448,256]{2,1,0:T(8,128)(2,1)S(1)} %get-tuple-element.9), channel_id=1, source_target_pairs={{0,4},{4,8},{8,12},{12,16},{16,20},{20,24},{24,28},{28,0},{1,5},{5... | collective-permute-start | bytes 688136 | tf_op jit(solution)/shard_map/ppermute | solution.py:22
  86.5 38.1 %collective-permute-start.5 = (bf16[1,448,256]{2,1,0:T(8,128)(2,1)S(1)}, bf16[1,448,256]{2,1,0:T(8,128)(2,1)S(1)}, u32[]{:S(2)}, u32[]{:S(2)}) collective-permute-start(bf16[1,448,256]{2,1,0:T(8,128)(2,1)S(1)} %get-tuple-element.10), channel_id=1, source_target_pairs={{0,8},{4,12},{8,16},{12,20},{16,24},{20,28},{24,0},{28,4},{1,9},{5... | collective-permute-start | bytes 688136 | tf_op jit(solution)/shard_map/ppermute | solution.py:22
  87.5 37.0 %collective-permute-start.4 = (bf16[1,448,256]{2,1,0:T(8,128)(2,1)S(1)}, bf16[1,448,256]{2,1,0:T(8,128)(2,1)S(1)}, u32[]{:S(2)}, u32[]{:S(2)}) collective-permute-start(bf16[1,448,256]{2,1,0:T(8,128)(2,1)S(1)} %get-tuple-element.11), channel_id=1, source_target_pairs={{0,12},{4,16},{8,20},{12,24},{16,28},{20,0},{24,4},{28,8},{1,13},{... | collective-permute-start | bytes 688136 | tf_op jit(solution)/shard_map/ppermute | solution.py:22
  91.4 19.7 %collective-permute-start.2 = (bf16[1,448,256]{2,1,0:T(8,128)(2,1)S(1)}, bf16[1,448,256]{2,1,0:T(8,128)(2,1)S(1)}, u32[]{:S(2)}, u32[]{:S(2)}) collective-permute-start(bf16[1,448,256]{2,1,0:T(8,128)(2,1)S(1)} %get-tuple-element.13), channel_id=1, source_target_pairs={{0,20},{4,24},{8,28},{12,0},{16,4},{20,8},{24,12},{28,16},{1,21},{... | collective-permute-start | bytes 688136 | tf_op jit(solution)/shard_map/ppermute | solution.py:22
  96.4 28.1 %collective-permute-start.3 = (bf16[1,448,256]{2,1,0:T(8,128)(2,1)S(1)}, bf16[1,448,256]{2,1,0:T(8,128)(2,1)S(1)}, u32[]{:S(2)}, u32[]{:S(2)}) collective-permute-start(bf16[1,448,256]{2,1,0:T(8,128)(2,1)S(1)} %get-tuple-element.12), channel_id=1, source_target_pairs={{0,16},{4,20},{8,24},{12,28},{16,0},{20,4},{24,8},{28,12},{1,17},{... | collective-permute-start | bytes 688136 | tf_op jit(solution)/shard_map/ppermute | solution.py:22
  148.1 87.8 %all-to-all-start = ((bf16[16,448,256]{2,1,0:T(8,128)(2,1)}), bf16[16,448,256]{2,1,0:T(8,128)(2,1)}, u32[]{:S(2)}, u32[]{:S(2)}) async-start(bf16[16,448,256]{2,1,0:T(8,128)(2,1)} %broadcast_select_fusion), calls=%async_computation.1 | async-start | bytes 7340032 | tf_op jit(solution)/shard_map/all_to_all | solution.py:45
Sparse Core Ops, SparseCore 0:
  10.5 67.2 reduce-scatter.1
